TPU v7x, 32 devices: a whole 2x2x4 slice. The times are simulated.
32 devices in a mesh: ia: 4 (over z), ja: 8 (over y, x, core).
Axes of the slice: x: 2, y: 2, z: 4, core: 2. Of those that a mesh axis runs over, the one named last changes fastest.
Arguments:
- pno_basis: bfloat16 [4, 16, 512, 128], P('ia', 'ja'), may hold values from -0.4375 to 0.4375
- domain_map: int32 [4, 16, 512], replicated, may hold values from 0 to 1023, as said below
- amplitudes: float32 [4, 16, 128, 128], P('ia', 'ja'), may hold values from -6 to 6
- exchange_ints: float32 [4, 16, 128, 128], P('ia', 'ja'), may hold values from -6 to 6
- pno_energy: float32 [4, 16, 128], P('ia', 'ja'), may hold values from 0.5 to 3
- row_energy: float32 [4], P('ia'), may hold values from -1.5 to -0.3
- column_energy: float32 [16], P('ja'), may hold values from -1.5 to -0.3
- coupling_rows: float32 [4, 4], P('ia'), may hold values from -0.6 to 0.6
- coupling_columns: float32 [16, 16], P(None, 'ja'), may hold values from -0.6 to 0.6
- row_neighbours: int32 [4, 16, 3], P('ia', 'ja'), may hold values from 0 to 3, as said below
- column_neighbours: int32 [4, 16, 15], P('ia', 'ja'), may hold values from 0 to 15, as said below
- row_counts: int32 [4, 16], P('ia', 'ja'), may hold values from 1 to 3
- column_counts: int32 [4, 16], P('ia', 'ja'), may hold values from 1 to 15
Outputs:
- new_amplitudes: float32 [4, 16, 128, 128], P('ia', 'ja')
- pair_energy: float32 [4, 16], P('ia', 'ja')
Inputs may be any that keep to these rules, and one draw needn't show every extreme that they name: `domain_map`: the 512 entries of one pair are distinct. `row_neighbours`: the 3 entries of a pair (i, j) are distinct and differ from i. `column_neighbours`: the 15 entries of a pair (i, j) are distinct and differ from j.
All inputs are finite; a program needn't handle non-finite values.
Results may differ from a plain program's by a relative error of at most 0.008.
Values may be sent and summed in bfloat16 or wider, within the bound.
A program may use at most 64 MiB of HBM per device.

v0:
```python
import jax
import jax.numpy as jnp
from jax import lax
from jax.sharding import PartitionSpec as P

ITERS = 2
level_shift = 0.3


def pair_intersections(packed):
    own_domain, own_basis, partner_domains, partner_bases = packed
    match = (own_domain[None, :, None] == partner_domains[:, None, :]).astype(jnp.bfloat16)
    picked = jnp.einsum(
        "suv,svb->sub", match, partner_bases, preferred_element_type=jnp.float32
    ).astype(jnp.bfloat16)
    return jnp.einsum("ua,sub->sab", own_basis, picked, preferred_element_type=jnp.float32).astype(
        jnp.bfloat16
    )


def local(
    pno_basis,
    domain_map,
    amplitudes,
    exchange_ints,
    pno_energy,
    row_energy,
    column_energy,
    coupling_rows,
    coupling_columns,
    row_neighbours,
    column_neighbours,
    row_counts,
    column_counts,
):
    pair_rows = pno_basis.shape[0]
    pair_columns = pno_basis.shape[1]
    domain_size = pno_basis.shape[2]
    width = amplitudes.shape[-1]
    total_rows = domain_map.shape[0]
    total_columns = domain_map.shape[1]
    own_pairs = pair_rows * pair_columns
    row_offset = lax.axis_index("ia") * pair_rows
    column_offset = lax.axis_index("ja") * pair_columns
    domain_rows = lax.dynamic_slice_in_dim(domain_map, row_offset, pair_rows, 0)
    domain_columns = lax.dynamic_slice_in_dim(domain_map, column_offset, pair_columns, 1)
    own_domain = lax.dynamic_slice_in_dim(domain_rows, column_offset, pair_columns, 1).reshape(
        own_pairs, domain_size
    )
    own_basis = pno_basis.reshape(own_pairs, domain_size, width)
    local_rows = jnp.arange(pair_rows, dtype=jnp.int32)[:, None, None]
    local_columns = jnp.arange(pair_columns, dtype=jnp.int32)[None, :, None]
    row_slots = (row_neighbours * pair_columns + local_columns).reshape(own_pairs, -1)
    column_slots = (local_rows * total_columns + column_neighbours).reshape(own_pairs, -1)
    row_live = (
        jnp.arange(row_neighbours.shape[2], dtype=jnp.int32)[None, None, :] < row_counts[:, :, None]
    )
    row_table = jnp.broadcast_to(coupling_rows[:, None, :], (pair_rows, pair_columns, total_rows))
    row_weight = jnp.where(row_live, jnp.take_along_axis(row_table, row_neighbours, axis=2), 0.0)
    column_live = (
        jnp.arange(column_neighbours.shape[2], dtype=jnp.int32)[None, None, :]
        < column_counts[:, :, None]
    )
    column_table = coupling_columns.T[None, :, :]
    column_weight = jnp.where(
        column_live, jnp.take_along_axis(column_table, column_neighbours, axis=2), 0.0
    )
    weights = jnp.concatenate(
        [row_weight.reshape(own_pairs, -1), column_weight.reshape(own_pairs, -1)], axis=1
    )
    partner_domains = jnp.concatenate(
        [
            domain_columns.reshape(total_rows * pair_columns, domain_size)[row_slots],
            domain_rows.reshape(pair_rows * total_columns, domain_size)[column_slots],
        ],
        axis=1,
    )

    def slot_pick(column_slab, row_slab):
        column_flat = column_slab.reshape(
            (column_slab.shape[0] * column_slab.shape[1],) + column_slab.shape[2:]
        )
        row_flat = row_slab.reshape((row_slab.shape[0] * row_slab.shape[1],) + row_slab.shape[2:])
        return jnp.concatenate([column_flat[row_slots], row_flat[column_slots]], axis=1)

    energy_gap = (
        pno_energy[:, :, :, None]
        + pno_energy[:, :, None, :]
        - row_energy[:, None, None, None]
        - column_energy[None, :, None, None]
    )
    current = amplitudes
    for iteration in range(ITERS):
        rounded = current.astype(jnp.bfloat16)
        column_bases, column_rounded = (
            lax.all_gather(pno_basis, "ia", axis=0, tiled=True),
            lax.all_gather(rounded, "ia", axis=0, tiled=True),
        )
        row_bases, row_rounded = (
            lax.all_gather(pno_basis, "ja", axis=1, tiled=True),
            lax.all_gather(rounded, "ja", axis=1, tiled=True),
        )
        partner_bases = slot_pick(column_bases, row_bases)
        intersections = lax.map(
            pair_intersections, (own_domain, own_basis, partner_domains, partner_bases)
        )
        intersection_wide = intersections.astype(jnp.float32)
        halved = jnp.einsum(
            "psab,psbc->psac",
            intersection_wide,
            slot_pick(column_rounded, row_rounded).astype(jnp.float32),
        ).astype(jnp.bfloat16)
        projected = jnp.einsum("psac,psdc->psad", halved.astype(jnp.float32), intersection_wide)
        coupled = jnp.sum(weights[:, :, None, None] * projected, axis=1).reshape(
            pair_rows, pair_columns, width, width
        )
        residual = exchange_ints + energy_gap * current - coupled
        current = current - residual / (energy_gap + level_shift)
    pair_energy = jnp.sum(
        exchange_ints * (2.0 * current - jnp.swapaxes(current, 2, 3)), axis=(2, 3)
    )
    return (current, pair_energy)


def solution(mesh):
    in_specs = (
        P("ia", "ja", None, None),
        P(),
        P("ia", "ja", None, None),
        P("ia", "ja", None, None),
        P("ia", "ja", None),
        P("ia"),
        P("ja"),
        P("ia", None),
        P(None, "ja"),
        P("ia", "ja", None),
        P("ia", "ja", None),
        P("ia", "ja"),
        P("ia", "ja"),
    )
    out_specs = (P("ia", "ja", None, None), P("ia", "ja"))
    return jax.shard_map(local, mesh=mesh, in_specs=in_specs, out_specs=out_specs, check_vma=False)
```

profile of v0, /device:TPU:0, one launch (start us, length us, event | category | flops | bytes accessed | tf_op | source)
XLA Modules:
  0.0 133.0 jit_solution(14398114743911281365)
XLA Ops:
  7.2 0.7 all-gather.3.cloned.1.call-update
  8.0 0.7 all-gather.5.cloned.1.call-update
  8.7 0.7 bitcast_or_fusion
  9.5 0.6 gather_fusion.1
  10.9 11.3 %all_gather.23 = bf16[1,16,128,128]{3,2,0,1:T(8,128)(2,1)S(1)} all-gather(bf16[1,2,128,128]{3,2,0,1:T(8,128)(2,1)S(1)} %convert_bitcast_fusion), channel_id=1, replica_groups=mesh['ia'=4,'ja'=8] {'ja'}, dimensions={1}, use_global_device_ids=true | all-gather | bytes 589824 | tf_op jit(solution)/shard_map/all_gather | solution.py:101
  22.3 0.7 gather_fusion.5
  23.0 16.9 %all_gather.22 = bf16[4,2,128,128]{3,2,1,0:T(8,128)(2,1)S(1)} all-gather(bf16[1,2,128,128]{3,2,1,0:T(8,128)(2,1)S(1)} %convert_element_type.21), channel_id=1, replica_groups=mesh['ia'=4,'ja'=8] {'ia'}, dimensions={0}, use_global_device_ids=true | all-gather | bytes 327680 | tf_op jit(solution)/shard_map/all_gather | solution.py:97
  40.6 0.7 gather_fusion.8
  41.4 0.9 gather_fusion.9
  43.4 1.1 all-gather.3.cloned.1.call-done
  44.5 1.9 %gather_fusion.2 = bf16[6,512,128]{2,1,0:T(8,128)(2,1)S(1)} fusion(bf16[8,512,128]{2,1,0:T(8,128)(2,1)} %bitcast.122, s32[1024]{0:T(1024)S(1)} %pad_clamp_fusion.1), kind=kCustom, calls=%fused_computation.2 | custom fusion | bytes 1572888 | tf_op jit(solution)/shard_map/gather | solution.py:84
  46.5 27.1 %all-gather.5.cloned.1.call-done = bf16[1,16,512,128]{3,2,0,1:T(8,128)(2,1)} async-done(((bf16[1,2,512,128]{3,2,0,1:T(8,128)(2,1)}), bf16[1,16,512,128]{3,2,0,1:T(8,128)(2,1)}) %all-gather.5.cloned.1.call-update) | async-done | bytes 2097168 | tf_op jit(solution)/shard_map/all_gather | solution.py:100
  73.6 4.6 %gather_fusion.3 = bf16[30,512,128]{2,1,0:T(8,128)(2,1)} fusion(bf16[16,512,128]{2,1,0:T(8,128)(2,1)} %bitcast.111, s32[1024]{0:T(1024)S(1)} %pad_clamp_fusion), kind=kCustom, calls=%fused_computation.3 | custom fusion | bytes 7864440 | tf_op jit(solution)/shard_map/gather | solution.py:84
  78.2 4.7 %pad_maximum_fusion = bf16[2,18,512,128]{3,2,1,0:T(8,128)(2,1)} fusion(bf16[2,15,512,128]{3,2,1,0:T(8,128)(2,1)} %bitcast.110, bf16[2,3,512,128]{3,2,1,0:T(8,128)(2,1)S(1)} %bitcast.114), kind=kLoop, calls=%fused_computation.26 | loop fusion | flops 2359296 | bytes 9437184 | tf_op jit(solution)/shard_map/concatenate | solution.py:84
  82.9 11.8 %while.2 = (s32[]{:T(128)}, bf16[2,18,128,128]{2,3,1,0:T(8,128)(2,1)}, s32[2,512]{1,0:T(2,128)S(1)}, s32[2,18,512]{2,1,0:T(8,128)S(1)}, bf16[2,18,512,128]{3,2,1...) while((s32[]{:T(128)}, bf16[2,18,128,128]{2,3,1,0:T(8,128)(2,1)}, s32[2,512]{1,0:T(2,128)S(1)}, ...), condition=%wide.region_1.2_spmd, body=%wide.region_0.0_spmd.sunk | while | flops 1516142592 | bytes 3210837 | solution.py:104
  82.9 5.9 %fusion.81 = bf16[2,18,128,128]{2,3,1,0:T(8,128)(2,1)} fusion(bf16[2,18,128,128]{2,3,1,0:T(8,128)(2,1)} %get-tuple-element.110, s32[]{:T(128)} %get-tuple-element.109, bf16[2,18,512,128]{3,2,1,0:T(8,128)(2,1)} %get-tuple-element.120, s32[18,512]{1,0:T(8,128)S(1)} %dynamic-slice_bitcast_fusion.4, s32[512]{0:T(512)S(1)} %bitcast.125, ...), kind=kOutput, calls=%fused_computation.20.clone.1 | convolution fusion | flops 1516142592 | bytes 3132928 | tf_op jit(solution)/shard_map/while/body/eval_jaxpr/ua,sub->sab/dot_general | solution.py:16
  88.9 5.8 %fusion.81 = bf16[2,18,128,128]{2,3,1,0:T(8,128)(2,1)} fusion(bf16[2,18,128,128]{2,3,1,0:T(8,128)(2,1)} %get-tuple-element.110, s32[]{:T(128)} %get-tuple-element.109, bf16[2,18,512,128]{3,2,1,0:T(8,128)(2,1)} %get-tuple-element.120, s32[18,512]{1,0:T(8,128)S(1)} %dynamic-slice_bitcast_fusion.4, s32[512]{0:T(512)S(1)} %bitcast.125, ...), kind=kOutput, calls=%fused_computation.20.clone.1 | convolution fusion | flops 1516142592 | bytes 3132928 | tf_op jit(solution)/shard_map/while/body/eval_jaxpr/ua,sub->sab/dot_general | solution.py:16
  94.7 2.6 %multiply_reduce_fusion.1 = f32[2,128,128]{2,1,0:T(8,128)S(1)} fusion(bf16[2,18,128,128]{2,3,1,0:T(8,128)(2,1)} %get-tuple-element.40, bf16[2,15,128,128]{3,2,1,0:T(8,128)(2,1)S(1)} %bitcast.117, bf16[2,3,128,128]{3,2,1,0:T(8,128)(2,1)S(1)} %bitcast.123, f32[2,18]{1,0:T(2,128)S(1)} %pad_maximum_fusion.1), kind=kOutput, calls=%fused_computation.28 | convolution fusion | flops 304316416 | bytes 2490512 | tf_op jit(solution)/shard_map/psac,psdc->psad/dot_general | solution.py:113
  97.5 13.9 %all_gather.24 = bf16[4,2,128,128]{3,2,1,0:T(8,128)(2,1)S(1)} all-gather(bf16[1,2,128,128]{3,2,1,0:T(8,128)(2,1)S(1)} %get-tuple-element.59), channel_id=1, replica_groups=mesh['ia'=4,'ja'=8] {'ia'}, dimensions={0}, use_global_device_ids=true | all-gather | bytes 327680 | tf_op jit(solution)/shard_map/all_gather | solution.py:97
  111.5 9.8 %all_gather.25 = bf16[1,16,128,128]{3,2,0,1:T(8,128)(2,1)S(1)} all-gather(bf16[1,2,128,128]{3,2,0,1:T(8,128)(2,1)S(1)} %bitcast.121), channel_id=1, replica_groups=mesh['ia'=4,'ja'=8] {'ja'}, dimensions={1}, use_global_device_ids=true | all-gather | bytes 589824 | tf_op jit(solution)/shard_map/all_gather | solution.py:101
  121.3 0.7 gather_fusion.7
  122.0 0.6 gather_fusion.6
  122.6 2.6 %multiply_reduce_fusion = f32[2,128,128]{2,1,0:T(8,128)S(1)} fusion(bf16[2,18,128,128]{2,3,1,0:T(8,128)(2,1)} %get-tuple-element.40, bf16[2,15,128,128]{3,2,1,0:T(8,128)(2,1)S(1)} %bitcast.118, bf16[2,3,128,128]{3,2,1,0:T(8,128)(2,1)S(1)} %bitcast.124, f32[2,18]{1,0:T(2,128)S(1)} %pad_maximum_fusion.1), kind=kOutput, calls=%fused_computation.27 | convolution fusion | flops 304316416 | bytes 2490512 | tf_op jit(solution)/shard_map/psac,psdc->psad/dot_general | solution.py:113
  125.5 0.6 fusion.54
  (61 shorter events, 2.6 us)
Async XLA Ops:
  7.2 2.3 %copy-start = (s32[4,16,512]{2,1,0:T(8,128)S(1)}, s32[4,16,512]{2,1,0:T(8,128)}, u32[]{:S(2)}) copy-start(s32[4,16,512]{2,1,0:T(8,128)} %param.16) | copy-start | bytes 393220
  7.2 3.0 %copy-start.7 = (s32[1,2,3]{2,1,0:T(2,128)S(1)}, s32[1,2,3]{2,1,0:T(2,128)}, u32[]{:S(2)}) copy-start(s32[1,2,3]{2,1,0:T(2,128)} %param.24) | copy-start | bytes 76
  7.2 3.7 %copy-start.2 = (f32[1,2,128,128]{3,2,1,0:T(8,128)S(1)}, f32[1,2,128,128]{3,2,1,0:T(8,128)}, u32[]{:S(2)}) copy-start(f32[1,2,128,128]{3,2,1,0:T(8,128)} %param.17) | copy-start | bytes 393220
  7.2 37.3 %all-gather.3.cloned.1.call-start = ((), (), s32[]{:S(2)}) async-start(), calls=%async_computation | async-start | bytes 1310720 | tf_op jit(solution)/shard_map/all_gather | solution.py:96
  7.9 65.7 %all-gather.5.cloned.1.call-start = ((), (), s32[]{:S(2)}) async-start(), calls=%async_computation.1 | async-start | bytes 2359296 | tf_op jit(solution)/shard_map/all_gather | solution.py:100
  22.3 18.3 %copy-start.12 = (f32[1,4]{1,0:T(1,128)S(1)}, f32[1,4]{1,0:T(1,128)}, u32[]{:S(2)}) copy-start(f32[1,4]{1,0:T(1,128)} %param.22) | copy-start | bytes 52
  23.0 18.4 %copy-start.1 = (f32[16,2]{0,1:T(2,128)S(1)}, f32[16,2]{0,1:T(2,128)}, u32[]{:S(2)}) copy-start(f32[16,2]{0,1:T(2,128)} %param.23) | copy-start | bytes 388
  39.9 3.1 %copy-start.4 = (f32[1,2,128,128]{3,2,1,0:T(8,128)S(1)}, f32[1,2,128,128]{3,2,1,0:T(8,128)}, u32[]{:S(2)}) copy-start(f32[1,2,128,128]{3,2,1,0:T(8,128)} %param.18) | copy-start | bytes 393220
  40.6 2.6 %copy-start.10 = (s32[1,2]{1,0:T(1,128)S(1)}, s32[1,2]{1,0:T(1,128)}, u32[]{:S(2)}) copy-start(s32[1,2]{1,0:T(1,128)} %param.26) | copy-start | bytes 28
  40.6 2.7 %copy-start.8 = (s32[1,2,15]{2,1,0:T(2,128)S(1)}, s32[1,2,15]{2,1,0:T(2,128)}, u32[]{:S(2)}) copy-start(s32[1,2,15]{2,1,0:T(2,128)} %param.25) | copy-start | bytes 364
  40.6 2.6 %copy-start.11 = (s32[1,2]{1,0:T(1,128)S(1)}, s32[1,2]{1,0:T(1,128)}, u32[]{:S(2)}) copy-start(s32[1,2]{1,0:T(1,128)} %param.27) | copy-start | bytes 28
  78.2 4.7 %copy-start.5 = (bf16[1,2,512,128]{3,2,1,0:T(8,128)(2,1)S(1)}, bf16[1,2,512,128]{3,2,1,0:T(8,128)(2,1)}, u32[]{:S(2)}) copy-start(bf16[1,2,512,128]{3,2,1,0:T(8,128)(2,1)} %param.15) | copy-start | bytes 786436
  94.7 2.7 %copy-start.6 = (f32[1,2,128]{2,1,0:T(2,128)S(1)}, f32[1,2,128]{2,1,0:T(2,128)}, u32[]{:S(2)}) copy-start(f32[1,2,128]{2,1,0:T(2,128)} %param.19) | copy-start | bytes 3076
  94.7 2.7 %copy-start.9 = (f32[2]{0:T(128)S(1)}, f32[2]{0:T(128)}, u32[]{:S(2)}) copy-start(f32[2]{0:T(128)} %param.21) | copy-start | bytes 28
  125.4 0.8 copy-start.3
Sparse Core Ops, SparseCore 0:
  9.6 34.9 all-gather.2
  46.4 27.1 all-gather.4
where the time goes:
time: 133 us
  blocking collectives  51.9 us (39%)
  waiting for transfers between devices  29.6 us (22%)
  matrix products  17 us (13%)
  between operations  15 us (11%)
  local copies, waits for them, and re-layouts  12.7 us (10%)
  other arithmetic  6.59 us (5%)
    all_gather x2, blocking collectives, local(): lax.all_gather(rounded, 'ia', axis=0, tiled=True)  30.8 us
    all_gather x1, waiting for transfers between devices, local(): lax.all_gather(pno_basis, 'ja', axis=1, tiled=True)  27.1 us
    all_gather x2, blocking collectives, local(): lax.all_gather(rounded, 'ja', axis=1, tiled=True)  21.1 us
    dot_general x2, matrix products, pair_intersections(): jnp.einsum('ua,sub->sab', own_basis, picked, preferred_element_type=jnp.f...  11.8 us
    gather x3, local copies, waits for them, and re-layouts, slot_pick(): row_flat[column_slots]  6.08 us
    dot_general x2, matrix products, local(): jnp.einsum('psac,psdc->psad', halved.astype(jnp.float32), intersection_wide)  5.29 us
    concatenate x1, other arithmetic, slot_pick(): jnp.concatenate([column_flat[row_slots], row_flat[column_slots]], axis=1)  4.69 us
    gather x3, local copies, waits for them, and re-layouts, slot_pick(): column_flat[row_slots]  3.09 us
  transfers between devices with their start and end apart: 2, of which 2 were waited for; matrix products, arithmetic and copies ran while one was open for 6% of the time, Pallas kernels for 0%

commit v1 on v0

--- a/solution.py
+++ b/solution.py
@@ -98,7 +98,7 @@
         )
         row_bases, row_rounded = (
             lax.all_gather(pno_basis, "ja", axis=1, tiled=True),
-            lax.all_gather(rounded, "ja", axis=1, tiled=True),
+            jnp.concatenate(lax.all_gather(rounded, "ja"), axis=1),
         )
         partner_bases = slot_pick(column_bases, row_bases)
         intersections = lax.map(

time: 133 us -> 133 us (level)
  no operation moved by 1% of the time
where the time goes in v1:
time: 133 us
  blocking collectives  52 us (39%)
  waiting for transfers between devices  29.7 us (22%)
  matrix products  17 us (13%)
  between operations  15 us (11%)
  local copies, waits for them, and re-layouts  12.7 us (10%)
  other arithmetic  6.56 us (5%)
    all_gather x2, blocking collectives, local(): lax.all_gather(rounded, 'ia', axis=0, tiled=True)  30.9 us
    all_gather x1, waiting for transfers between devices, local(): lax.all_gather(pno_basis, 'ja', axis=1, tiled=True)  27.1 us
    all_gather x2, blocking collectives, local(): lax.all_gather(rounded, 'ja')  21.1 us
    dot_general x2, matrix products, pair_intersections(): jnp.einsum('ua,sub->sab', own_basis, picked, preferred_element_type=jnp.f...  11.8 us
    gather x3, local copies, waits for them, and re-layouts, slot_pick(): row_flat[column_slots]  6.08 us
    dot_general x2, matrix products, local(): jnp.einsum('psac,psdc->psad', halved.astype(jnp.float32), intersection_wide)  5.28 us
    concatenate x1, other arithmetic, slot_pick(): jnp.concatenate([column_flat[row_slots], row_flat[column_slots]], axis=1)  4.69 us
    gather x3, local copies, waits for them, and re-layouts, slot_pick(): column_flat[row_slots]  3.09 us
  transfers between devices with their start and end apart: 2, of which 2 were waited for; matrix products, arithmetic and copies ran while one was open for 6% of the time, Pallas kernels for 0%

profile of v1, /device:TPU:0, one launch (start us, length us, event | category | flops | bytes accessed | tf_op | source)
XLA Modules:
  0.0 133.1 jit_solution(12470380145079233270)
XLA Ops:
  7.2 0.7 all-gather.5.cloned.1.call-update
  8.0 0.7 all-gather.7.cloned.1.call-update
  8.7 0.7 bitcast_or_fusion
  9.5 0.6 gather_fusion.1
  10.9 11.3 %all-gather = bf16[8,2,128,128]{3,2,1,0:T(8,128)(2,1)S(1)} all-gather(bf16[1,2,128,128]{3,2,1,0:T(8,128)(2,1)S(1)} %convert_element_type.21), channel_id=2, replica_groups=mesh['ia'=4,'ja'=8] {'ja'}, dimensions={0}, use_global_device_ids=true | all-gather | bytes 589824 | tf_op jit(solution)/shard_map/all_gather | solution.py:101
  22.2 0.7 gather_fusion.5
  23.0 16.9 %all_gather.28 = bf16[4,2,128,128]{3,2,1,0:T(8,128)(2,1)S(1)} all-gather(bf16[1,2,128,128]{3,2,1,0:T(8,128)(2,1)S(1)} %convert_element_type.21), channel_id=1, replica_groups=mesh['ia'=4,'ja'=8] {'ia'}, dimensions={0}, use_global_device_ids=true | all-gather | bytes 327680 | tf_op jit(solution)/shard_map/all_gather | solution.py:97
  40.6 0.7 gather_fusion.8
  41.4 0.9 gather_fusion.9
  43.4 1.1 all-gather.5.cloned.1.call-done
  44.5 1.9 %gather_fusion.2 = bf16[6,512,128]{2,1,0:T(8,128)(2,1)S(1)} fusion(bf16[8,512,128]{2,1,0:T(8,128)(2,1)} %bitcast.118, s32[1024]{0:T(1024)S(1)} %pad_clamp_fusion.1), kind=kCustom, calls=%fused_computation.2 | custom fusion | bytes 1572888 | tf_op jit(solution)/shard_map/gather | solution.py:84
  46.5 27.1 %all-gather.7.cloned.1.call-done = bf16[1,16,512,128]{3,2,0,1:T(8,128)(2,1)} async-done(((bf16[1,2,512,128]{3,2,0,1:T(8,128)(2,1)}), bf16[1,16,512,128]{3,2,0,1:T(8,128)(2,1)}) %all-gather.7.cloned.1.call-update) | async-done | bytes 2097168 | tf_op jit(solution)/shard_map/all_gather | solution.py:100
  73.6 4.6 %gather_fusion.3 = bf16[30,512,128]{2,1,0:T(8,128)(2,1)} fusion(bf16[16,512,128]{2,1,0:T(8,128)(2,1)} %bitcast.108, s32[1024]{0:T(1024)S(1)} %pad_clamp_fusion), kind=kCustom, calls=%fused_computation.3 | custom fusion | bytes 7864440 | tf_op jit(solution)/shard_map/gather | solution.py:84
  78.2 4.7 %pad_maximum_fusion = bf16[2,18,512,128]{3,2,1,0:T(8,128)(2,1)} fusion(bf16[2,15,512,128]{3,2,1,0:T(8,128)(2,1)} %bitcast.107, bf16[2,3,512,128]{3,2,1,0:T(8,128)(2,1)S(1)} %bitcast.111), kind=kLoop, calls=%fused_computation.26 | loop fusion | flops 2359296 | bytes 9437184 | tf_op jit(solution)/shard_map/concatenate | solution.py:84
  82.9 11.8 %while.2 = (s32[]{:T(128)}, bf16[2,18,128,128]{2,3,1,0:T(8,128)(2,1)}, s32[2,512]{1,0:T(2,128)S(1)}, s32[2,18,512]{2,1,0:T(8,128)S(1)}, bf16[2,18,512,128]{3,2,1...) while((s32[]{:T(128)}, bf16[2,18,128,128]{2,3,1,0:T(8,128)(2,1)}, s32[2,512]{1,0:T(2,128)S(1)}, ...), condition=%wide.region_1.2_spmd, body=%wide.region_0.0_spmd.sunk | while | flops 1516142592 | bytes 3210837 | solution.py:104
  82.9 5.9 %fusion.81 = bf16[2,18,128,128]{2,3,1,0:T(8,128)(2,1)} fusion(bf16[2,18,128,128]{2,3,1,0:T(8,128)(2,1)} %get-tuple-element.110, s32[]{:T(128)} %get-tuple-element.109, bf16[2,18,512,128]{3,2,1,0:T(8,128)(2,1)} %get-tuple-element.120, s32[18,512]{1,0:T(8,128)S(1)} %dynamic-slice_bitcast_fusion.4, s32[512]{0:T(512)S(1)} %bitcast.121, ...), kind=kOutput, calls=%fused_computation.20.clone.1 | convolution fusion | flops 1516142592 | bytes 3132928 | tf_op jit(solution)/shard_map/while/body/eval_jaxpr/ua,sub->sab/dot_general | solution.py:16
  88.9 5.8 %fusion.81 = bf16[2,18,128,128]{2,3,1,0:T(8,128)(2,1)} fusion(bf16[2,18,128,128]{2,3,1,0:T(8,128)(2,1)} %get-tuple-element.110, s32[]{:T(128)} %get-tuple-element.109, bf16[2,18,512,128]{3,2,1,0:T(8,128)(2,1)} %get-tuple-element.120, s32[18,512]{1,0:T(8,128)S(1)} %dynamic-slice_bitcast_fusion.4, s32[512]{0:T(512)S(1)} %bitcast.121, ...), kind=kOutput, calls=%fused_computation.20.clone.1 | convolution fusion | flops 1516142592 | bytes 3132928 | tf_op jit(solution)/shard_map/while/body/eval_jaxpr/ua,sub->sab/dot_general | solution.py:16
  94.7 2.6 %multiply_reduce_fusion.1 = f32[2,128,128]{2,1,0:T(8,128)S(1)} fusion(bf16[2,18,128,128]{2,3,1,0:T(8,128)(2,1)} %get-tuple-element.40, bf16[2,15,128,128]{3,2,1,0:T(8,128)(2,1)S(1)} %bitcast.114, bf16[2,3,128,128]{3,2,1,0:T(8,128)(2,1)S(1)} %bitcast.119, f32[2,18]{1,0:T(2,128)S(1)} %pad_maximum_fusion.1), kind=kOutput, calls=%fused_computation.28 | convolution fusion | flops 304316416 | bytes 2490512 | tf_op jit(solution)/shard_map/psac,psdc->psad/dot_general | solution.py:113
  97.5 9.8 %all-gather.1 = bf16[8,2,128,128]{3,2,1,0:T(8,128)(2,1)S(1)} all-gather(bf16[1,2,128,128]{3,2,1,0:T(8,128)(2,1)S(1)} %get-tuple-element.59), channel_id=3, replica_groups=mesh['ia'=4,'ja'=8] {'ja'}, dimensions={0}, use_global_device_ids=true | all-gather | bytes 589824 | tf_op jit(solution)/shard_map/all_gather | solution.py:101
  107.3 14.0 %all_gather.31 = bf16[4,2,128,128]{3,2,1,0:T(8,128)(2,1)S(1)} all-gather(bf16[1,2,128,128]{3,2,1,0:T(8,128)(2,1)S(1)} %get-tuple-element.59), channel_id=1, replica_groups=mesh['ia'=4,'ja'=8] {'ia'}, dimensions={0}, use_global_device_ids=true | all-gather | bytes 327680 | tf_op jit(solution)/shard_map/all_gather | solution.py:97
  121.3 0.7 gather_fusion.7
  122.1 0.6 gather_fusion.6
  122.7 2.6 %multiply_reduce_fusion = f32[2,128,128]{2,1,0:T(8,128)S(1)} fusion(bf16[2,18,128,128]{2,3,1,0:T(8,128)(2,1)} %get-tuple-element.40, bf16[2,15,128,128]{3,2,1,0:T(8,128)(2,1)S(1)} %bitcast.115, bf16[2,3,128,128]{3,2,1,0:T(8,128)(2,1)S(1)} %bitcast.120, f32[2,18]{1,0:T(2,128)S(1)} %pad_maximum_fusion.1), kind=kOutput, calls=%fused_computation.27 | convolution fusion | flops 304316416 | bytes 2490512 | tf_op jit(solution)/shard_map/psac,psdc->psad/dot_general | solution.py:113
  125.6 0.6 fusion.54
  (60 shorter events, 2.6 us)
Async XLA Ops:
  7.2 2.3 %copy-start = (s32[4,16,512]{2,1,0:T(8,128)S(1)}, s32[4,16,512]{2,1,0:T(8,128)}, u32[]{:S(2)}) copy-start(s32[4,16,512]{2,1,0:T(8,128)} %param.16) | copy-start | bytes 393220
  7.2 3.0 %copy-start.7 = (s32[1,2,3]{2,1,0:T(2,128)S(1)}, s32[1,2,3]{2,1,0:T(2,128)}, u32[]{:S(2)}) copy-start(s32[1,2,3]{2,1,0:T(2,128)} %param.24) | copy-start | bytes 76
  7.2 3.7 %copy-start.5 = (f32[1,2,128,128]{3,2,1,0:T(8,128)S(1)}, f32[1,2,128,128]{3,2,1,0:T(8,128)}, u32[]{:S(2)}) copy-start(f32[1,2,128,128]{3,2,1,0:T(8,128)} %param.17) | copy-start | bytes 393220
  7.2 37.3 %all-gather.5.cloned.1.call-start = ((), (), s32[]{:S(2)}) async-start(), calls=%async_computation | async-start | bytes 1310720 | tf_op jit(solution)/shard_map/all_gather | solution.py:96
  7.9 65.7 %all-gather.7.cloned.1.call-start = ((), (), s32[]{:S(2)}) async-start(), calls=%async_computation.1 | async-start | bytes 2359296 | tf_op jit(solution)/shard_map/all_gather | solution.py:100
  22.2 18.3 %copy-start.12 = (f32[1,4]{1,0:T(1,128)S(1)}, f32[1,4]{1,0:T(1,128)}, u32[]{:S(2)}) copy-start(f32[1,4]{1,0:T(1,128)} %param.22) | copy-start | bytes 52
  23.0 18.4 %copy-start.1 = (f32[16,2]{0,1:T(2,128)S(1)}, f32[16,2]{0,1:T(2,128)}, u32[]{:S(2)}) copy-start(f32[16,2]{0,1:T(2,128)} %param.23) | copy-start | bytes 388
  39.9 3.1 %copy-start.3 = (f32[1,2,128,128]{3,2,1,0:T(8,128)S(1)}, f32[1,2,128,128]{3,2,1,0:T(8,128)}, u32[]{:S(2)}) copy-start(f32[1,2,128,128]{3,2,1,0:T(8,128)} %param.18) | copy-start | bytes 393220
  40.5 2.6 %copy-start.10 = (s32[1,2]{1,0:T(1,128)S(1)}, s32[1,2]{1,0:T(1,128)}, u32[]{:S(2)}) copy-start(s32[1,2]{1,0:T(1,128)} %param.26) | copy-start | bytes 28
  40.6 2.7 %copy-start.8 = (s32[1,2,15]{2,1,0:T(2,128)S(1)}, s32[1,2,15]{2,1,0:T(2,128)}, u32[]{:S(2)}) copy-start(s32[1,2,15]{2,1,0:T(2,128)} %param.25) | copy-start | bytes 364
  40.6 2.6 %copy-start.11 = (s32[1,2]{1,0:T(1,128)S(1)}, s32[1,2]{1,0:T(1,128)}, u32[]{:S(2)}) copy-start(s32[1,2]{1,0:T(1,128)} %param.27) | copy-start | bytes 28
  78.2 4.7 %copy-start.4 = (bf16[1,2,512,128]{3,2,1,0:T(8,128)(2,1)S(1)}, bf16[1,2,512,128]{3,2,1,0:T(8,128)(2,1)}, u32[]{:S(2)}) copy-start(bf16[1,2,512,128]{3,2,1,0:T(8,128)(2,1)} %param.15) | copy-start | bytes 786436
  94.7 2.7 %copy-start.6 = (f32[1,2,128]{2,1,0:T(2,128)S(1)}, f32[1,2,128]{2,1,0:T(2,128)}, u32[]{:S(2)}) copy-start(f32[1,2,128]{2,1,0:T(2,128)} %param.19) | copy-start | bytes 3076
  94.7 2.7 %copy-start.9 = (f32[2]{0:T(128)S(1)}, f32[2]{0:T(128)}, u32[]{:S(2)}) copy-start(f32[2]{0:T(128)} %param.21) | copy-start | bytes 28
  125.5 0.7 copy-start.2
Sparse Core Ops, SparseCore 0:
  9.6 34.9 all-gather.4
  46.4 27.1 all-gather.6
